TPU v7x, 32 devices: a whole 2x2x4 slice. The times are simulated.
32 devices in a mesh: slides: 2 (over y), rows: 4 (over z), cols: 2 (over x), chan: 2 (over core).
Axes of the slice: x: 2, y: 2, z: 4, core: 2. Of those that a mesh axis runs over, the one named last changes fastest.
Arguments:
- features: bfloat16 [128, 64, 384], P(('slides', 'rows'), 'cols', 'chan'), parts along dimension 0, may hold values from -6 to 6
- gate_input: bfloat16 [128, 64, 384], P(('slides', 'rows'), 'cols', 'chan'), parts along dimension 0, may hold values from -6 to 6
- decay_idx: int32 [128, 64], P(('slides', 'rows'), 'cols'), parts along dimension 0, may hold values from 0 to 15
- log_table: float32 [16, 384], P(None, 'chan'), may hold values from -1 to 0, as said below
- state_rate: float32 [16], replicated, may hold values from 0.5 to 2
- proj_row: bfloat16 [384, 32], P('chan'), may hold values from -0.0390625 to 0.0390625
- proj_col: bfloat16 [384, 32], P('chan'), may hold values from -0.0390625 to 0.0390625
- conv_w: float32 [3, 3, 384], P(None, None, 'chan'), may hold values from -0.5 to 0.5
- conv_b: float32 [384], P('chan'), may hold values from -0.5 to 0.5
- d_skip: float32 [384], P('chan'), may hold values from 0.5 to 1.5
Outputs:
- output: bfloat16 [128, 64, 384], P(('slides', 'rows'), 'cols', 'chan'), parts along dimension 0
There are 2 independent parts, one for each index of `slides`. A program takes and returns all parts, laid end to end along the dimension named above; an argument that names none is the same for every part. Nothing has to cross between parts.
Inputs may be any that keep to these rules, and one draw needn't show every extreme that they name: `log_table`: every entry is negative.
All inputs are finite; a program needn't handle non-finite values.
Results may differ from a plain program's by a relative error of at most 0.0061.
Values may be sent and summed in bfloat16 or wider, within the bound.
No kernel may reach another device: no remote copies, remote signals or barrier semaphores. Data moves between devices by JAX's collectives and lax.ppermute only.
A program may use at most 128 MiB of HBM per device.

v0:
```python
import jax
import jax.numpy as jnp
from jax import lax
from jax.sharding import PartitionSpec as P


def entering(shard, axis, combine, identity):
    size, position = (lax.axis_size(axis), lax.axis_index(axis))
    everything = jax.tree.map(lambda part: lax.all_gather(part, axis), shard)
    start = jax.tree.map(
        lambda part, zero: jnp.broadcast_to(jnp.asarray(zero, part.dtype), part.shape),
        shard,
        identity,
    )

    def step(k, before):
        reached = k < position
        new = combine(before, jax.tree.map(lambda part: part[k], everything))
        return jax.tree.map(lambda a, b: jnp.where(reached, a, b), new, before)

    return lax.fori_loop(0, size, step, start)


def extended(block, sides, width):
    for axis, dim in sides:
        count = lax.axis_size(axis)
        forward = [(i, i + 1) for i in range(count - 1)]
        backward = [(target, source) for source, target in forward]
        low = lax.ppermute(
            lax.slice_in_dim(block, block.shape[dim] - width, None, axis=dim), axis, forward
        )
        high = lax.ppermute(lax.slice_in_dim(block, 0, width, axis=dim), axis, backward)
        block = jnp.concatenate([low, block, high], axis=dim)
    return block


def combine_pair(earlier, latter):
    return (earlier[0] + latter[0], latter[1] + jnp.exp(latter[0]) * earlier[1])


def make_carry_combine(state_rate):
    rates = state_rate[:, None, None]

    def combine_carry(earlier, latter):
        return (earlier[0] + latter[0], latter[1] + jnp.exp(rates * latter[0][None]) * earlier[1])

    return combine_carry


def lookup(decay_idx, log_table):
    entries = log_table.shape[0]
    onehot = (decay_idx[..., None] == jnp.arange(entries, dtype=jnp.int32)).astype(jnp.float32)
    return jnp.einsum("hwk,ke->hwe", onehot, log_table, precision=lax.Precision.HIGHEST)


def tile_states(values, log_decays, coeffs, state_rate, scan_axis):
    num_states = state_rate.shape[0]
    drive_cols = jnp.moveaxis(coeffs[..., :num_states], -1, 0)[..., None]
    log_sums = jnp.cumsum(log_decays, axis=scan_axis)

    def one_state(inputs):
        state_scale, drive_col = inputs
        unused, states = lax.associative_scan(
            combine_pair, (log_decays * state_scale, drive_col * values), axis=scan_axis
        )
        return states

    return (log_sums, lax.map(one_state, (state_rate, drive_cols)))


def finish(log_sums, states, inflow, coeffs, state_rate):
    num_states = states.shape[0]
    outputs = jnp.moveaxis(coeffs[..., num_states:], -1, 0)[..., None]
    carried = jnp.exp(state_rate[:, None, None, None] * log_sums[None]) * inflow
    return jnp.sum(outputs * (states + carried), axis=0)


def column_coeffs(middle, proj_col):
    return lax.psum(jnp.dot(middle, proj_col, preferred_element_type=jnp.float32), "chan")


def shards(
    features,
    gate_input,
    decay_idx,
    log_table,
    state_rate,
    proj_row,
    proj_col,
    conv_w,
    conv_b,
    d_skip,
):
    combine_carry = make_carry_combine(state_rate)
    log_decays = lookup(decay_idx, log_table)
    feats_wide = features.astype(jnp.float32)
    coeff_row = lax.psum(jnp.dot(features, proj_row, preferred_element_type=jnp.float32), "chan")
    row_sums, states = tile_states(feats_wide, log_decays, coeff_row, state_rate, 1)
    tile_ends = (row_sums[:, -1, :], states[:, :, -1, :])
    incoming = entering(
        tile_ends,
        "cols",
        combine_carry,
        (jnp.zeros_like(tile_ends[0]), jnp.zeros_like(tile_ends[1])),
    )
    swept_rows = finish(row_sums, states, incoming[1][:, :, None, :], coeff_row, state_rate)
    row_out = (swept_rows + d_skip * feats_wide).astype(jnp.bfloat16)
    padded = extended(row_out, (("rows", 0), ("cols", 1)), 1).astype(jnp.float32)
    tile_rows = row_out.shape[0]
    tile_cols = row_out.shape[1]
    convolved = jnp.zeros(row_out.shape, jnp.float32) + conv_b
    for offset_row in range(3):
        for offset_col in range(3):
            convolved = (
                convolved
                + conv_w[offset_row, offset_col]
                * padded[offset_row : offset_row + tile_rows, offset_col : offset_col + tile_cols]
            )
    middle = jax.nn.silu(convolved).astype(jnp.bfloat16)
    strip_vals = lax.all_to_all(middle, "rows", split_axis=1, concat_axis=0, tiled=True)
    strip_index = lax.all_to_all(decay_idx, "rows", split_axis=1, concat_axis=0, tiled=True)
    strip_decays = lookup(strip_index, log_table)
    strip_wide = strip_vals.astype(jnp.float32)
    coeff_col = column_coeffs(strip_vals, proj_col)
    col_sums, states = tile_states(strip_wide, strip_decays, coeff_col, state_rate, 0)
    strip_out = (
        finish(col_sums, states, jnp.zeros((), jnp.float32), coeff_col, state_rate)
        + d_skip * strip_wide
    )
    combined = lax.all_to_all(strip_out, "rows", split_axis=0, concat_axis=1, tiled=True)
    return (combined * jax.nn.silu(gate_input.astype(jnp.float32))).astype(jnp.bfloat16)


def solution(mesh):
    placed = (
        P(("slides", "rows"), "cols", "chan"),
        P(("slides", "rows"), "cols", "chan"),
        P(("slides", "rows"), "cols"),
        P(None, "chan"),
        P(),
        P("chan", None),
        P("chan", None),
        P(None, None, "chan"),
        P("chan"),
        P("chan"),
    )
    return jax.shard_map(
        shards,
        mesh=mesh,
        in_specs=placed,
        out_specs=P(("slides", "rows"), "cols", "chan"),
        check_vma=False,
    )
```

profile of v0, /device:TPU:0, one launch (start us, length us, event | category | flops | bytes accessed | tf_op | source)
XLA Modules:
  0.0 399.4 jit_solution(8053558625621068115)
XLA Ops:
  6.5 1.9 fusion.42
  9.9 6.3 %all-to-all-start.1 = ((s32[4,1,128]{2,1,0:T(1,128)}), s32[4,1,128]{2,1,0:T(1,128)S(1)}, u32[]{:S(2)}, u32[]{:S(2)}) async-start(s32[4,1,128]{2,1,0:T(1,128)} %reshape.23), calls=%async_computation.1 | async-start | bytes 4096 | tf_op jit(solution)/shard_map/all_to_all | solution.py:121
  17.8 1.8 convert_element_type.23
  20.7 4.4 %all-gather.1 = f32[32,1,192]{2,0,1:T(8,128)S(1)} all-gather(f32[16,1,192]{2,0,1:T(8,128)S(1)} %slice.400), channel_id=3, replica_groups=mesh['slides'=2,'rows'=4,'cols'=2,'chan'=2] {'cols'}, dimensions={0}, use_global_device_ids=true | all-gather | bytes 36864 | tf_op jit(solution)/shard_map/all_gather | solution.py:9
  25.1 5.5 %all-reduce.25.cloned.1.call-done = f32[16,32,32]{2,1,0:T(8,128)} async-done(((f32[16,32,32]{2,1,0:T(8,128)}), f32[16,32,32]{2,1,0:T(8,128)}) %all-reduce.25.cloned.1.call-update) | async-done | bytes 65552 | tf_op jit(solution)/shard_map/psum | solution.py:97
  30.6 1.9 slice_bitcast_fusion.3
  33.3 179.7 %while.37 = (s32[]{:T(128)}, f32[16,16,32,192]{3,2,1,0:T(8,128)}, f32[16,16,32,1]{2,1,3,0:T(8,128)}, f32[16,32,192]{2,1,0:T(8,128)}, f32[16]{0:T(128)}, /*index=5*/f32[16,32,192]{2,1,0:T(8,128)S(1)}) while((s32[]{:T(128)}, f32[16,16,32,192]{3,2,1,0:T(8,128)}, f32[16,16,32,1]{2,1,3,0:T(8,128)}, f32[16,32,192]{2,1,0:T(8,128)}, ...), condition=%wide.region_2.3_spmd.clone, body=%wide.region_1.0_spmd.sunk.clone | while | flops 998402 | bytes 15030905 | solution.py:68
  34.0 1.3 dynamic_slice.48
  35.3 1.9 broadcast_multiply_fusion.8
  45.2 1.3 dynamic_slice.48
  46.5 1.9 broadcast_multiply_fusion.8
  57.8 1.9 broadcast_multiply_fusion.8
  67.7 1.3 dynamic_slice.48
  69.0 1.9 broadcast_multiply_fusion.8
  80.2 1.9 broadcast_multiply_fusion.8
  90.1 1.3 dynamic_slice.48
  91.4 1.9 broadcast_multiply_fusion.8
  101.3 1.3 dynamic_slice.48
  102.6 1.9 broadcast_multiply_fusion.8
  112.6 1.3 dynamic_slice.48
  113.9 1.9 broadcast_multiply_fusion.8
  123.8 1.3 dynamic_slice.48
  125.1 1.9 broadcast_multiply_fusion.8
  135.0 1.3 dynamic_slice.48
  136.3 1.9 broadcast_multiply_fusion.8
  146.2 1.3 dynamic_slice.48
  147.5 1.9 broadcast_multiply_fusion.8
  158.8 1.9 broadcast_multiply_fusion.8
  170.0 1.9 broadcast_multiply_fusion.8
  179.9 1.3 dynamic_slice.48
  181.2 1.9 broadcast_multiply_fusion.8
  192.4 1.9 broadcast_multiply_fusion.8
  203.7 1.9 broadcast_multiply_fusion.8
  212.9 9.9 %copy.50 = f32[16,16,32,192]{3,1,2,0:T(8,128)S(1)} copy(f32[16,16,32,192]{3,2,1,0:T(8,128)} %get-tuple-element.178) | data formatting | bytes 12582912 | tf_op jit(solution)/shard_map/while | solution.py:68
  223.0 9.5 %all-gather = f32[32,16,1,192]{3,1,2,0:T(8,128)S(1)} all-gather(f32[16,16,1,192]{3,1,2,0:T(8,128)S(1)} %slice.399), channel_id=2, replica_groups=mesh['slides'=2,'rows'=4,'cols'=2,'chan'=2] {'cols'}, dimensions={0}, use_global_device_ids=true | all-gather | bytes 589824 | tf_op jit(solution)/shard_map/all_gather | solution.py:9
  232.9 4.8 %multiply_reduce_fusion.1 = f32[16,32,192]{2,1,0:T(8,128)S(1)} fusion(f32[16,16,32,192]{3,2,1,0:T(8,128)} %get-tuple-element.178, f32[16,16,192]{2,1,0:T(8,128)S(1)} %get-tuple-element.179, f32[16,32,192]{2,1,0:T(8,128)S(1)} %copy-done.4, f32[16]{0:T(128)S(1)} %bitcast.166, f32[16,16,32]{2,1,0:T(8,128)S(1)} %copy.46), kind=kLoop, calls=%fused_computation.70 | loop fusion | flops 7766016 | bytes 7307328 | tf_op jit(solution)/shard_map/reduce_sum | solution.py:75
  237.9 3.7 collective-permute-start
  244.2 3.0 collective-permute-done.1
  247.2 3.4 collective-permute-start.2
  252.0 4.2 %collective-permute-done.3 = bf16[18,1,192]{2,1,0:T(2,128)(2,1)S(1)} collective-permute-done((bf16[18,1,192]{2,1,0:T(2,128)(2,1)S(1)}, bf16[18,1,192]{2,1,0:T(2,128)(2,1)S(1)}, u32[]{:S(2)}, u32[]{:S(2)}) %collective-permute-start.3) | collective-permute-done | bytes 6944 | tf_op jit(solution)/shard_map/ppermute | solution.py:32
  257.8 3.7 all-to-all-start
  262.8 5.4 %all-to-all-done = bf16[16,32,192]{2,0,1:T(8,128)(2,1)S(1)} async-done(((bf16[16,32,192]{2,0,1:T(8,128)(2,1)}), bf16[16,32,192]{2,0,1:T(8,128)(2,1)S(1)}, u32[]{:S(2)}, u32[]{:S(2)}) %all-to-all-start) | async-done | bytes 196640 | tf_op jit(solution)/shard_map/all_to_all | solution.py:120
  269.3 17.2 %all-reduce.27.cloned.1.call-done = f32[64,8,32]{2,1,0:T(8,128)} async-done(((f32[64,8,32]{2,1,0:T(8,128)}), f32[64,8,32]{2,1,0:T(8,128)}) %all-reduce.27.cloned.1.call-update) | async-done | bytes 65552 | tf_op jit(solution)/shard_map/psum | solution.py:79
  286.5 1.9 slice_bitcast_fusion.1
  289.6 76.2 %while.38 = (s32[]{:T(128)}, f32[16,64,8,192]{3,2,1,0:T(8,128)}, f32[16,64,8,1]{2,1,3,0:T(8,128)}, f32[64,8,192]{2,1,0:T(8,128)S(1)}, f32[16]{0:T(128)S(1)}, /*index=5*/f32[64,8,192]{2,1,0:T(8,128)S(1)}) while((s32[]{:T(128)}, f32[16,64,8,192]{3,2,1,0:T(8,128)}, f32[16,64,8,1]{2,1,3,0:T(8,128)}, f32[64,8,192]{2,1,0:T(8,128)S(1)}, ...), condition=%wide.region_9.10_spmd.clone, body=%wide.region_8.9_spmd.sunk.clone | while | flops 1035266 | bytes 11215489 | solution.py:68
  365.8 1.5 copy.53
  367.3 4.7 %multiply_reduce_fusion = f32[64,8,192]{2,1,0:T(8,128)S(1)} fusion(f32[16,64,8,192]{3,2,1,0:T(8,128)} %get-tuple-element.180, f32[64,8,192]{2,1,0:T(8,128)} %fusion.52, f32[16]{0:T(128)S(1)} %get-tuple-element.646, f32[16,64,8]{2,1,0:T(8,128)S(1)} %copy.53), kind=kLoop, calls=%fused_computation.69 | loop fusion | flops 7766016 | bytes 7110720 | tf_op jit(solution)/shard_map/reduce_sum | solution.py:75
  372.1 19.6 %all_to_all.52 = f32[64,8,192]{2,1,0:T(8,128)S(1)} all-to-all(f32[64,8,192]{2,1,0:T(8,128)S(1)} %multiply_add_fusion.9), channel_id=1, replica_groups=mesh['slides'=2,'rows'=4,'cols'=2,'chan'=2] {'rows'}, dimensions={0} | all-to-all | bytes 786432 | tf_op jit(solution)/shard_map/all_to_all | solution.py:130
  (1533 shorter events, 218.9 us)
Async XLA Ops:
  6.5 9.7 %copy-start = (f32[16,192]{1,0:T(8,128)S(1)}, f32[16,192]{1,0:T(8,128)}, u32[]{:S(2)}) copy-start(f32[16,192]{1,0:T(8,128)} %param.19) | copy-start | bytes 36868
  6.5 24.1 %all-reduce.25.cloned.1.call-start = ((), (), s32[]{:S(2)}) async-start(), calls=%async_computation.3 | async-start | bytes 524288 | tf_op jit(solution)/shard_map/psum | solution.py:97
  9.9 233.0 %all-to-all-start.1 = ((s32[4,1,128]{2,1,0:T(1,128)}), s32[4,1,128]{2,1,0:T(1,128)S(1)}, u32[]{:S(2)}, u32[]{:S(2)}) async-start(s32[4,1,128]{2,1,0:T(1,128)} %reshape.23), calls=%async_computation.1 | async-start | bytes 4096 | tf_op jit(solution)/shard_map/all_to_all | solution.py:121
  212.9 19.5 %copy-start.7 = (f32[16]{0:T(128)S(1)}, f32[16]{0:T(128)}, u32[]{:S(2)}) copy-start(f32[16]{0:T(128)} %get-tuple-element.644) | copy-start | bytes 196
  212.9 19.8 %copy-start.5 = (f32[16,16,32]{0,2,1:T(8,128)S(1)}, f32[16,16,32]{0,2,1:T(8,128)}, u32[]{:S(2)}) copy-start(f32[16,16,32]{0,2,1:T(8,128)} %get-tuple-element.321) | copy-start | bytes 98308
  212.9 20.0 %copy-start.4 = (f32[16,32,192]{2,1,0:T(8,128)S(1)}, f32[16,32,192]{2,1,0:T(8,128)}, u32[]{:S(2)}) copy-start(f32[16,32,192]{2,1,0:T(8,128)} %copy.49) | copy-start | bytes 1179652
  222.9 14.9 %copy-start.3 = (bf16[16,32,192]{2,1,0:T(8,128)(2,1)S(1)}, bf16[16,32,192]{2,1,0:T(8,128)(2,1)}, u32[]{:S(2)}) copy-start(bf16[16,32,192]{2,1,0:T(8,128)(2,1)} %param.16) | copy-start | bytes 589828
  222.9 14.9 %copy-start.10 = (f32[192]{0:T(256)S(1)}, f32[192]{0:T(256)}, u32[]{:S(2)}) copy-start(f32[192]{0:T(256)} %param.25) | copy-start | bytes 2308
  222.9 19.9 %copy-start.9 = (f32[3,3,192]{2,1,0:T(4,128)S(1)}, f32[3,3,192]{2,1,0:T(4,128)}, u32[]{:S(2)}) copy-start(f32[3,3,192]{2,1,0:T(4,128)} %param.23) | copy-start | bytes 20740
  232.4 24.0 %copy-start.11 = (f32[192]{0:T(256)S(1)}, f32[192]{0:T(256)}, u32[]{:S(2)}) copy-start(f32[192]{0:T(256)} %param.24) | copy-start | bytes 2308
  232.9 35.4 %copy-start.8 = (bf16[192,32]{0,1:T(8,128)(2,1)S(1)}, bf16[192,32]{0,1:T(8,128)(2,1)}, u32[]{:S(2)}) copy-start(bf16[192,32]{0,1:T(8,128)(2,1)} %param.22) | copy-start | bytes 36868
  237.9 6.3 %collective-permute-start = (bf16[1,32,192]{2,1,0:T(8,128)(2,1)S(1)}, bf16[1,32,192]{2,1,0:T(8,128)(2,1)S(1)}, u32[]{:S(2)}, u32[]{:S(2)}) collective-permute-start(bf16[1,32,192]{2,1,0:T(8,128)(2,1)S(1)} %get-tuple-element.319), channel_id=1, source_target_pairs={{0,4},{4,8},{8,12},{1,5},{5,9},{9,13},{2,6},{6,10},{10,14},{3,7},{... | collective-permute-start | bytes 36872 | tf_op jit(solution)/shard_map/ppermute | solution.py:29
  241.5 5.6 %collective-permute-start.1 = (bf16[1,32,192]{2,1,0:T(8,128)(2,1)S(1)}, bf16[1,32,192]{2,1,0:T(8,128)(2,1)S(1)}, u32[]{:S(2)}, u32[]{:S(2)}) collective-permute-start(bf16[1,32,192]{2,1,0:T(8,128)(2,1)S(1)} %get-tuple-element.320), channel_id=1, source_target_pairs={{4,0},{8,4},{12,8},{5,1},{9,5},{13,9},{6,2},{10,6},{14,10},{7,3},{... | collective-permute-start | bytes 36872 | tf_op jit(solution)/shard_map/ppermute | solution.py:32
  247.2 4.8 %collective-permute-start.2 = (bf16[18,1,192]{2,1,0:T(2,128)(2,1)S(1)}, bf16[18,1,192]{2,1,0:T(2,128)(2,1)S(1)}, u32[]{:S(2)}, u32[]{:S(2)}) collective-permute-start(bf16[18,1,192]{2,1,0:T(2,128)(2,1)S(1)} %get-tuple-element.315), channel_id=1, source_target_pairs={{0,2},{1,3},{4,6},{5,7},{8,10},{9,11},{12,14},{13,15},{16,18},{17,... | collective-permute-start | bytes 20744 | tf_op jit(solution)/shard_map/ppermute | solution.py:29
  250.6 5.7 %collective-permute-start.3 = (bf16[18,1,192]{2,1,0:T(2,128)(2,1)S(1)}, bf16[18,1,192]{2,1,0:T(2,128)(2,1)S(1)}, u32[]{:S(2)}, u32[]{:S(2)}) collective-permute-start(bf16[18,1,192]{2,1,0:T(2,128)(2,1)S(1)} %get-tuple-element.316), channel_id=1, source_target_pairs={{2,0},{3,1},{6,4},{7,5},{10,8},{11,9},{14,12},{15,13},{18,16},{19,... | collective-permute-start | bytes 20744 | tf_op jit(solution)/shard_map/ppermute | solution.py:32
  257.8 10.5 %all-to-all-start = ((bf16[16,32,192]{2,0,1:T(8,128)(2,1)}), bf16[16,32,192]{2,0,1:T(8,128)(2,1)S(1)}, u32[]{:S(2)}, u32[]{:S(2)}) async-start(bf16[16,32,192]{2,0,1:T(8,128)(2,1)} %copy.51), calls=%async_computation | async-start | bytes 524288 | tf_op jit(solution)/shard_map/all_to_all | solution.py:120
  261.4 25.0 %all-reduce.27.cloned.1.call-start = ((), (), s32[]{:S(2)}) async-start(), calls=%async_computation.4 | async-start | bytes 524288 | tf_op jit(solution)/shard_map/psum | solution.py:79
  268.3 21.3 %copy-start.1 = (bf16[16,4,8,192]{3,2,0,1:T(8,128)(2,1)}, bf16[16,4,8,192]{3,2,0,1:T(8,128)(2,1)S(1)}, u32[]{:S(2)}) copy-start(bf16[16,4,8,192]{3,2,0,1:T(8,128)(2,1)S(1)} %copy.52) | copy-start | bytes 589828
  365.8 6.2 %copy-start.2 = (bf16[16,4,8,192]{3,2,0,1:T(8,128)(2,1)S(1)}, bf16[16,4,8,192]{3,2,0,1:T(8,128)(2,1)}, u32[]{:S(2)}) copy-start(bf16[16,4,8,192]{3,2,0,1:T(8,128)(2,1)} %copy-done.1) | copy-start | bytes 589828
  365.8 25.9 %copy-start.6 = (bf16[16,32,192]{2,1,0:T(8,128)(2,1)S(1)}, bf16[16,32,192]{2,1,0:T(8,128)(2,1)}, u32[]{:S(2)}) copy-start(bf16[16,32,192]{2,1,0:T(8,128)(2,1)} %param.17) | copy-start | bytes 589828
Sparse Core Ops, SparseCore 0:
  9.7 20.9 all-reduce.24
  269.4 17.0 all-reduce.26
where the time goes:
time: 403 us; the launch traced here: 399 us
  local copies, waits for them, and re-layouts  178 us (44%)
  other arithmetic  104 us (26%)
  waiting for transfers between devices  35.4 us (9%)
  blocking collectives  33.5 us (8%)
  starting transfers between devices  19.6 us (5%)
  between operations  13.7 us (3%)
  loops' own time  10.1 us (3%)
  matrix products  4.34 us (1%)
    slice x464, local copies, waits for them, and re-layouts, one_state(): lax.associative_scan(combine_pair, (log_decays * state_scale, drive_col *...  66 us
    mul x32, other arithmetic, one_state(): log_decays * state_scale  41.8 us
    pad x288, local copies, waits for them, and re-layouts, one_state(): lax.associative_scan(combine_pair, (log_decays * state_scale, drive_col *...  36.8 us
    dynamic_slice x32, local copies, waits for them, and re-layouts, tile_states(): return (log_sums, lax.map(one_state, (state_rate, drive_cols)))  30.6 us
    dynamic_update_slice x32, other arithmetic, tile_states(): return (log_sums, lax.map(one_state, (state_rate, drive_cols)))  28.1 us
    mul x32, local copies, waits for them, and re-layouts, one_state(): drive_col * values  23.3 us
    all_to_all x1, blocking collectives, shards(): lax.all_to_all(strip_out, 'rows', split_axis=0, concat_axis=1, tiled=True)  19.6 us
    psum x1, waiting for transfers between devices, column_coeffs(): lax.psum(jnp.dot(middle, proj_col, preferred_element_type=jnp.float32), '...  17.2 us
  transfers between devices with their start and end apart: 8, of which 6 were waited for; matrix products, arithmetic and copies ran while one was open for 50% of the time, Pallas kernels for 0%

commit v1 on v0

--- a/solution.py
+++ b/solution.py
@@ -76,7 +76,10 @@
 
 
 def column_coeffs(middle, proj_col):
-    return lax.psum(jnp.dot(middle, proj_col, preferred_element_type=jnp.float32), "chan")
+    return jnp.sum(
+        lax.all_gather(jnp.dot(middle, proj_col, preferred_element_type=jnp.float32), "chan"),
+        axis=0,
+    )
 
 
 def shards(

time: 403 us -> 383 us (0.950)
  waiting for transfers between devices: 35.4 us -> 18.2 us
    psum x1 -> x0, waiting for transfers between devices: 17.2 us -> none  [column_coeffs(): lax.psum(jnp.dot(middle, proj_col, preferred_element_type=jnp.float32), '...]
  transfers between devices with their start and end apart: 8 -> 7, of which waited for: 6 -> 5; matrix products, arithmetic and copies ran while one was open for 50% -> 52% of each run, Pallas kernels for 0% -> 0%
where the time goes in v1:
time: 383 us; the launch traced here: 379 us
  local copies, waits for them, and re-layouts  177 us (46%)
  other arithmetic  103 us (27%)
  blocking collectives  34.1 us (9%)
  starting transfers between devices  19.6 us (5%)
  waiting for transfers between devices  18.2 us (5%)
  between operations  13.7 us (4%)
  loops' own time  10.1 us (3%)
    slice x464, local copies, waits for them, and re-layouts, one_state(): lax.associative_scan(combine_pair, (log_decays * state_scale, drive_col *...  66 us
    mul x32, other arithmetic, one_state(): log_decays * state_scale  40.4 us
    pad x288, local copies, waits for them, and re-layouts, one_state(): lax.associative_scan(combine_pair, (log_decays * state_scale, drive_col *...  36.8 us
    dynamic_slice x32, local copies, waits for them, and re-layouts, tile_states(): return (log_sums, lax.map(one_state, (state_rate, drive_cols)))  29.3 us
    dynamic_update_slice x32, other arithmetic, tile_states(): return (log_sums, lax.map(one_state, (state_rate, drive_cols)))  28.1 us
    mul x32, local copies, waits for them, and re-layouts, one_state(): drive_col * values  23.3 us
    all_to_all x1, blocking collectives, shards(): lax.all_to_all(strip_out, 'rows', split_axis=0, concat_axis=1, tiled=True)  18 us
    all_gather x2, blocking collectives, entering(): everything = jax.tree.map(lambda part: lax.all_gather(part, axis), shard)  13.9 us
  transfers between devices with their start and end apart: 7, of which 5 were waited for; matrix products, arithmetic and copies ran while one was open for 52% of the time, Pallas kernels for 0%

profile of v1, /device:TPU:0, one launch (start us, length us, event | category | flops | bytes accessed | tf_op | source)
XLA Modules:
  0.0 379.1 jit_solution(2541651660457045248)
XLA Ops:
  6.5 1.9 fusion.42
  9.9 6.3 %all-to-all-start.1 = ((s32[4,1,128]{2,1,0:T(1,128)}), s32[4,1,128]{2,1,0:T(1,128)S(1)}, u32[]{:S(2)}, u32[]{:S(2)}) async-start(s32[4,1,128]{2,1,0:T(1,128)} %reshape.24), calls=%async_computation.1 | async-start | bytes 4096 | tf_op jit(solution)/shard_map/all_to_all | solution.py:124
  17.8 1.8 convert_element_type.23
  20.7 4.4 %all-gather.1 = f32[32,1,192]{2,0,1:T(8,128)S(1)} all-gather(f32[16,1,192]{2,0,1:T(8,128)S(1)} %slice.400), channel_id=3, replica_groups=mesh['slides'=2,'rows'=4,'cols'=2,'chan'=2] {'cols'}, dimensions={0}, use_global_device_ids=true | all-gather | bytes 36864 | tf_op jit(solution)/shard_map/all_gather | solution.py:9
  25.1 5.5 %all-reduce.24.cloned.1.call-done = f32[16,32,32]{2,1,0:T(8,128)} async-done(((f32[16,32,32]{2,1,0:T(8,128)}), f32[16,32,32]{2,1,0:T(8,128)}) %all-reduce.24.cloned.1.call-update) | async-done | bytes 65552 | tf_op jit(solution)/shard_map/psum | solution.py:100
  30.6 1.9 slice_bitcast_fusion.3
  33.3 177.3 %while.37 = (s32[]{:T(128)}, f32[16,16,32,192]{3,2,1,0:T(8,128)}, f32[16,16,32,1]{2,1,3,0:T(8,128)}, f32[16,32,192]{2,1,0:T(8,128)}, f32[16]{0:T(128)}, /*index=5*/f32[16,32,192]{2,1,0:T(8,128)S(1)}) while((s32[]{:T(128)}, f32[16,16,32,192]{3,2,1,0:T(8,128)}, f32[16,16,32,1]{2,1,3,0:T(8,128)}, f32[16,32,192]{2,1,0:T(8,128)}, ...), condition=%wide.region_2.3_spmd.clone, body=%wide.region_1.0_spmd.sunk.clone | while | flops 998402 | bytes 15030905 | solution.py:68
  34.0 1.2 dynamic_slice.48
  35.2 1.8 broadcast_multiply_fusion.8
  45.1 1.2 dynamic_slice.48
  46.3 1.8 broadcast_multiply_fusion.8
  57.4 1.8 broadcast_multiply_fusion.8
  68.5 1.8 broadcast_multiply_fusion.8
  78.3 1.2 dynamic_slice.48
  79.6 1.8 broadcast_multiply_fusion.8
  89.4 1.2 dynamic_slice.48
  90.6 1.8 broadcast_multiply_fusion.8
  101.7 1.8 broadcast_multiply_fusion.8
  111.5 1.2 dynamic_slice.48
  112.8 1.8 broadcast_multiply_fusion.8
  122.6 1.2 dynamic_slice.48
  123.8 1.8 broadcast_multiply_fusion.8
  133.7 1.2 dynamic_slice.48
  134.9 1.8 broadcast_multiply_fusion.8
  144.8 1.2 dynamic_slice.48
  146.0 1.8 broadcast_multiply_fusion.8
  155.8 1.2 dynamic_slice.48
  157.1 1.8 broadcast_multiply_fusion.8
  168.2 1.8 broadcast_multiply_fusion.8
  179.3 1.8 broadcast_multiply_fusion.8
  190.3 1.8 broadcast_multiply_fusion.8
  201.4 1.8 broadcast_multiply_fusion.8
  210.6 9.9 %copy.46 = f32[16,16,32,192]{3,1,2,0:T(8,128)S(1)} copy(f32[16,16,32,192]{3,2,1,0:T(8,128)} %get-tuple-element.178) | data formatting | bytes 12582912 | tf_op jit(solution)/shard_map/while | solution.py:68
  220.6 9.5 %all-gather = f32[32,16,1,192]{3,1,2,0:T(8,128)S(1)} all-gather(f32[16,16,1,192]{3,1,2,0:T(8,128)S(1)} %slice.399), channel_id=2, replica_groups=mesh['slides'=2,'rows'=4,'cols'=2,'chan'=2] {'cols'}, dimensions={0}, use_global_device_ids=true | all-gather | bytes 589824 | tf_op jit(solution)/shard_map/all_gather | solution.py:9
  230.6 4.8 %multiply_reduce_fusion.1 = f32[16,32,192]{2,1,0:T(8,128)S(1)} fusion(f32[16,16,32,192]{3,2,1,0:T(8,128)} %get-tuple-element.178, f32[16,16,192]{2,1,0:T(8,128)S(1)} %get-tuple-element.179, f32[16,32,192]{2,1,0:T(8,128)S(1)} %copy-done.4, f32[16]{0:T(128)S(1)} %bitcast.168, f32[16,16,32]{2,1,0:T(8,128)S(1)} %copy.42), kind=kLoop, calls=%fused_computation.70 | loop fusion | flops 7766016 | bytes 7307328 | tf_op jit(solution)/shard_map/reduce_sum | solution.py:75
  235.5 3.7 collective-permute-start
  239.2 1.3 collective-permute-start.1
  241.8 3.0 collective-permute-done.1
  244.8 3.4 collective-permute-start.2
  248.2 1.3 collective-permute-start.3
  249.7 4.2 %collective-permute-done.3 = bf16[18,1,192]{2,1,0:T(2,128)(2,1)S(1)} collective-permute-done((bf16[18,1,192]{2,1,0:T(2,128)(2,1)S(1)}, bf16[18,1,192]{2,1,0:T(2,128)(2,1)S(1)}, u32[]{:S(2)}, u32[]{:S(2)}) %collective-permute-start.3) | collective-permute-done | bytes 6944 | tf_op jit(solution)/shard_map/ppermute | solution.py:32
  255.4 3.7 all-to-all-start
  260.4 5.4 %all-to-all-done = bf16[16,32,192]{2,0,1:T(8,128)(2,1)S(1)} async-done(((bf16[16,32,192]{2,0,1:T(8,128)(2,1)}), bf16[16,32,192]{2,0,1:T(8,128)(2,1)S(1)}, u32[]{:S(2)}, u32[]{:S(2)}) %all-to-all-start) | async-done | bytes 196640 | tf_op jit(solution)/shard_map/all_to_all | solution.py:123
  266.8 2.2 all-gather.2
  271.1 75.9 %while.38 = (s32[]{:T(128)}, f32[16,64,8,192]{3,2,1,0:T(8,128)}, f32[16,64,8,1]{2,1,3,0:T(8,128)}, f32[64,8,192]{2,1,0:T(8,128)S(1)}, f32[16]{0:T(128)S(1)}, /*index=5*/f32[64,8,192]{2,1,0:T(8,128)S(1)}) while((s32[]{:T(128)}, f32[16,64,8,192]{3,2,1,0:T(8,128)}, f32[16,64,8,1]{2,1,3,0:T(8,128)}, f32[64,8,192]{2,1,0:T(8,128)S(1)}, ...), condition=%wide.region_9.10_spmd.clone, body=%wide.region_8.9_spmd.sunk.clone | while | flops 1035266 | bytes 11215489 | solution.py:68
  347.1 1.5 copy.49
  348.6 4.7 %multiply_reduce_fusion = f32[64,8,192]{2,1,0:T(8,128)S(1)} fusion(f32[16,64,8,192]{3,2,1,0:T(8,128)} %get-tuple-element.180, f32[64,8,192]{2,1,0:T(8,128)} %fusion.52, f32[16]{0:T(128)S(1)} %get-tuple-element.630, f32[16,64,8]{2,1,0:T(8,128)S(1)} %copy.49), kind=kLoop, calls=%fused_computation.69 | loop fusion | flops 7766016 | bytes 7110720 | tf_op jit(solution)/shard_map/reduce_sum | solution.py:75
  353.4 18.0 %all_to_all.52 = f32[64,8,192]{2,1,0:T(8,128)S(1)} all-to-all(f32[64,8,192]{2,1,0:T(8,128)S(1)} %multiply_add_fusion.9), channel_id=1, replica_groups=mesh['slides'=2,'rows'=4,'cols'=2,'chan'=2] {'rows'}, dimensions={0} | all-to-all | bytes 786432 | tf_op jit(solution)/shard_map/all_to_all | solution.py:133
  (1532 shorter events, 217.8 us)
Async XLA Ops:
  6.5 9.7 %copy-start = (f32[16,192]{1,0:T(8,128)S(1)}, f32[16,192]{1,0:T(8,128)}, u32[]{:S(2)}) copy-start(f32[16,192]{1,0:T(8,128)} %param.19) | copy-start | bytes 36868
  6.5 24.1 %all-reduce.24.cloned.1.call-start = ((), (), s32[]{:S(2)}) async-start(), calls=%async_computation.3 | async-start | bytes 524288 | tf_op jit(solution)/shard_map/psum | solution.py:100
  9.9 230.6 %all-to-all-start.1 = ((s32[4,1,128]{2,1,0:T(1,128)}), s32[4,1,128]{2,1,0:T(1,128)S(1)}, u32[]{:S(2)}, u32[]{:S(2)}) async-start(s32[4,1,128]{2,1,0:T(1,128)} %reshape.24), calls=%async_computation.1 | async-start | bytes 4096 | tf_op jit(solution)/shard_map/all_to_all | solution.py:124
  210.6 19.5 %copy-start.7 = (f32[16]{0:T(128)S(1)}, f32[16]{0:T(128)}, u32[]{:S(2)}) copy-start(f32[16]{0:T(128)} %get-tuple-element.628) | copy-start | bytes 196
  210.6 19.8 %copy-start.5 = (f32[16,16,32]{0,2,1:T(8,128)S(1)}, f32[16,16,32]{0,2,1:T(8,128)}, u32[]{:S(2)}) copy-start(f32[16,16,32]{0,2,1:T(8,128)} %get-tuple-element.309) | copy-start | bytes 98308
  210.6 20.0 %copy-start.4 = (f32[16,32,192]{2,1,0:T(8,128)S(1)}, f32[16,32,192]{2,1,0:T(8,128)}, u32[]{:S(2)}) copy-start(f32[16,32,192]{2,1,0:T(8,128)} %copy.45) | copy-start | bytes 1179652
  220.5 14.9 %copy-start.3 = (bf16[16,32,192]{2,1,0:T(8,128)(2,1)S(1)}, bf16[16,32,192]{2,1,0:T(8,128)(2,1)}, u32[]{:S(2)}) copy-start(bf16[16,32,192]{2,1,0:T(8,128)(2,1)} %param.16) | copy-start | bytes 589828
  220.5 14.9 %copy-start.10 = (f32[192]{0:T(256)S(1)}, f32[192]{0:T(256)}, u32[]{:S(2)}) copy-start(f32[192]{0:T(256)} %param.25) | copy-start | bytes 2308
  220.5 19.9 %copy-start.9 = (f32[3,3,192]{2,1,0:T(4,128)S(1)}, f32[3,3,192]{2,1,0:T(4,128)}, u32[]{:S(2)}) copy-start(f32[3,3,192]{2,1,0:T(4,128)} %param.23) | copy-start | bytes 20740
  230.0 24.0 %copy-start.11 = (f32[192]{0:T(256)S(1)}, f32[192]{0:T(256)}, u32[]{:S(2)}) copy-start(f32[192]{0:T(256)} %param.24) | copy-start | bytes 2308
  230.6 36.1 %copy-start.8 = (bf16[192,32]{0,1:T(8,128)(2,1)S(1)}, bf16[192,32]{0,1:T(8,128)(2,1)}, u32[]{:S(2)}) copy-start(bf16[192,32]{0,1:T(8,128)(2,1)} %param.22) | copy-start | bytes 36868
  235.5 6.3 %collective-permute-start = (bf16[1,32,192]{2,1,0:T(8,128)(2,1)S(1)}, bf16[1,32,192]{2,1,0:T(8,128)(2,1)S(1)}, u32[]{:S(2)}, u32[]{:S(2)}) collective-permute-start(bf16[1,32,192]{2,1,0:T(8,128)(2,1)S(1)} %get-tuple-element.307), channel_id=1, source_target_pairs={{0,4},{4,8},{8,12},{1,5},{5,9},{9,13},{2,6},{6,10},{10,14},{3,7},{... | collective-permute-start | bytes 36872 | tf_op jit(solution)/shard_map/ppermute | solution.py:29
  239.2 5.6 %collective-permute-start.1 = (bf16[1,32,192]{2,1,0:T(8,128)(2,1)S(1)}, bf16[1,32,192]{2,1,0:T(8,128)(2,1)S(1)}, u32[]{:S(2)}, u32[]{:S(2)}) collective-permute-start(bf16[1,32,192]{2,1,0:T(8,128)(2,1)S(1)} %get-tuple-element.308), channel_id=1, source_target_pairs={{4,0},{8,4},{12,8},{5,1},{9,5},{13,9},{6,2},{10,6},{14,10},{7,3},{... | collective-permute-start | bytes 36872 | tf_op jit(solution)/shard_map/ppermute | solution.py:32
  244.8 4.8 %collective-permute-start.2 = (bf16[18,1,192]{2,1,0:T(2,128)(2,1)S(1)}, bf16[18,1,192]{2,1,0:T(2,128)(2,1)S(1)}, u32[]{:S(2)}, u32[]{:S(2)}) collective-permute-start(bf16[18,1,192]{2,1,0:T(2,128)(2,1)S(1)} %get-tuple-element.303), channel_id=1, source_target_pairs={{0,2},{1,3},{4,6},{5,7},{8,10},{9,11},{12,14},{13,15},{16,18},{17,... | collective-permute-start | bytes 20744 | tf_op jit(solution)/shard_map/ppermute | solution.py:29
  248.2 5.7 %collective-permute-start.3 = (bf16[18,1,192]{2,1,0:T(2,128)(2,1)S(1)}, bf16[18,1,192]{2,1,0:T(2,128)(2,1)S(1)}, u32[]{:S(2)}, u32[]{:S(2)}) collective-permute-start(bf16[18,1,192]{2,1,0:T(2,128)(2,1)S(1)} %get-tuple-element.304), channel_id=1, source_target_pairs={{2,0},{3,1},{6,4},{7,5},{10,8},{11,9},{14,12},{15,13},{18,16},{19,... | collective-permute-start | bytes 20744 | tf_op jit(solution)/shard_map/ppermute | solution.py:32
  255.4 10.5 %all-to-all-start = ((bf16[16,32,192]{2,0,1:T(8,128)(2,1)}), bf16[16,32,192]{2,0,1:T(8,128)(2,1)S(1)}, u32[]{:S(2)}, u32[]{:S(2)}) async-start(bf16[16,32,192]{2,0,1:T(8,128)(2,1)} %copy.47), calls=%async_computation | async-start | bytes 524288 | tf_op jit(solution)/shard_map/all_to_all | solution.py:123
  265.9 0.7 copy-start.1
  347.1 6.2 %copy-start.2 = (bf16[16,4,8,192]{3,2,0,1:T(8,128)(2,1)S(1)}, bf16[16,4,8,192]{3,2,0,1:T(8,128)(2,1)}, u32[]{:S(2)}) copy-start(bf16[16,4,8,192]{3,2,0,1:T(8,128)(2,1)} %copy-done.1) | copy-start | bytes 589828
  347.1 24.3 %copy-start.6 = (bf16[16,32,192]{2,1,0:T(8,128)(2,1)S(1)}, bf16[16,32,192]{2,1,0:T(8,128)(2,1)}, u32[]{:S(2)}) copy-start(bf16[16,32,192]{2,1,0:T(8,128)(2,1)} %param.17) | copy-start | bytes 589828
Sparse Core Ops, SparseCore 0:
  9.7 20.9 all-reduce.23
